TPU v7x, 512 devices: a whole 4x4x16 slice. The times are simulated.
512 devices in a mesh: seq: 16 (over y, x), expert: 32 (over z, core).
Axes of the slice: x: 4, y: 4, z: 16, core: 2. Of those that a mesh axis runs over, the one named last changes fastest.
Arguments:
- tokens: bfloat16 [8192, 2048], P(('seq', 'expert')), may hold values from -6 to 6
- out_grads: bfloat16 [8192, 2048], P(('seq', 'expert')), may hold values from -6 to 6
- route_ids: int32 [8192, 6], P(('seq', 'expert')), may hold values from 0 to 63, all different within a row; in each aligned block of 16 rows (0 to 15, 16 to 31, ...) at most 2 rows name the same one
- route_probs: bfloat16 [8192, 6], P(('seq', 'expert')), may hold values from 0.049804688 to 1
- w_gate_up: bfloat16 [512, 2, 176, 2048], P(('seq', 'expert')), may hold values from -0.125 to 0.125
- w_down: bfloat16 [512, 176, 2048], P(('seq', 'expert')), may hold values from -0.15625 to 0.15625
Outputs:
- grad_tokens: bfloat16 [8192, 2048], P(('seq', 'expert'))
- grad_probs: float32 [8192, 6], P(('seq', 'expert'))
- grad_gate_up: bfloat16 [512, 2, 176, 2048], P(('seq', 'expert'))
- grad_down: bfloat16 [512, 176, 2048], P(('seq', 'expert'))
Inputs may be any that keep to these rules, and one draw needn't show every extreme that they name: `route_ids`: in the rows of one device (16 aligned rows) no expert is named by more than 2 routes, a bound that some block reaches; a token's 6 experts differ.
All inputs are finite; a program needn't handle non-finite values.
Results may differ from a plain program's by a relative error of at most 0.0065.
Values may be sent and summed in bfloat16 or wider, within the bound.
A program may use at most 64 MiB of HBM per device.

v0:
```python
import jax
import jax.numpy as jnp
from jax import lax
from jax.sharding import PartitionSpec as P


def slot_picks(route_ids, experts, capacity):
    rows, top = route_ids.shape
    flat = route_ids.reshape(rows * top)
    onehot = (flat[:, None] == jnp.arange(experts, dtype=jnp.int32)[None, :]).astype(jnp.int32)
    rank = jnp.sum((jnp.cumsum(onehot, axis=0) - onehot) * onehot, axis=1)
    target = flat * capacity + rank
    return jnp.arange(experts * capacity, dtype=jnp.int32)[:, None] == target[None, :]


def expert_side(xs, dys, weights, w_gate_up, w_down):
    w_gate = w_gate_up[0, 0]
    w_up = w_gate_up[0, 1]
    w_out = w_down[0]
    contract = (((1,), (1,)), ((), ()))
    gate = lax.dot_general(xs, w_gate, contract, preferred_element_type=jnp.float32)
    upper = lax.dot_general(xs, w_up, contract, preferred_element_type=jnp.float32)
    sig = jax.nn.sigmoid(gate)
    act = gate * sig * upper
    err = lax.dot_general(dys, w_out, contract, preferred_element_type=jnp.float32)
    score = jnp.sum(err * act, axis=1)
    weight = weights.astype(jnp.float32)[:, None]
    delta = weight * err
    grad_g = (delta * upper * sig * (1.0 + gate * (1.0 - sig))).astype(jnp.bfloat16)
    grad_u = (delta * gate * sig).astype(jnp.bfloat16)
    scaled = (weight * dys.astype(jnp.float32)).astype(jnp.bfloat16)
    inner = (((0,), (0,)), ((), ()))
    grad_gate = lax.dot_general(grad_g, xs, inner, preferred_element_type=jnp.float32).astype(
        jnp.bfloat16
    )
    grad_up = lax.dot_general(grad_u, xs, inner, preferred_element_type=jnp.float32).astype(
        jnp.bfloat16
    )
    grad_gu = jnp.stack([grad_gate, grad_up], 0)[None]
    grad_out = lax.dot_general(
        act.astype(jnp.bfloat16), scaled, inner, preferred_element_type=jnp.float32
    ).astype(jnp.bfloat16)[None]
    dx_part = jnp.dot(grad_g, w_gate, preferred_element_type=jnp.float32) + jnp.dot(
        grad_u, w_up, preferred_element_type=jnp.float32
    )
    return (dx_part, score, grad_gu, grad_out)


def body(tokens, out_grads, route_ids, route_probs, w_gate_up, w_down):
    rows, width = tokens.shape
    top = route_ids.shape[1]
    columns = lax.axis_size("expert")
    groups = lax.axis_size("seq")
    slices = columns // 4
    experts = groups * 4
    capacity = max(2, (rows * top * 4 // 3 + experts - 1) // experts)
    picks = slot_picks(route_ids, experts, capacity)
    token_pick = jnp.any(picks.reshape(experts * capacity, rows, top), axis=2).astype(jnp.bfloat16)
    pick_float = picks.astype(jnp.float32)
    send_x = jnp.dot(token_pick, tokens, preferred_element_type=jnp.float32).astype(jnp.bfloat16)
    send_dy = jnp.dot(token_pick, out_grads, preferred_element_type=jnp.float32).astype(
        jnp.bfloat16
    )
    send_p = jnp.sum(
        pick_float * route_probs.reshape(1, rows * top).astype(jnp.float32), axis=1
    ).astype(jnp.bfloat16)
    arrived = (
        lax.all_to_all(
            send_x.reshape(groups, 4 * capacity, width),
            "seq",
            split_axis=0,
            concat_axis=0,
            tiled=True,
        ),
        lax.all_to_all(
            send_dy.reshape(groups, 4 * capacity, width),
            "seq",
            split_axis=0,
            concat_axis=0,
            tiled=True,
        ),
        lax.all_to_all(
            send_p.reshape(groups, 4 * capacity), "seq", split_axis=0, concat_axis=0, tiled=True
        ),
    )
    arrived_x = arrived[0].reshape(groups, 4, capacity, width)
    arrived_dy = arrived[1].reshape(groups, 4, capacity, width)
    fan_p = jnp.repeat(jnp.moveaxis(arrived[2].reshape(groups, 4, capacity), 1, 0), slices, axis=0)
    total_rows = columns * groups * capacity
    fan_x = jnp.repeat(jnp.moveaxis(arrived_x, 1, 0), slices, axis=0)
    fan_dy = jnp.repeat(jnp.moveaxis(arrived_dy, 1, 0), slices, axis=0)
    got = (
        lax.all_to_all(fan_x, "expert", split_axis=0, concat_axis=0, tiled=True),
        lax.all_to_all(fan_dy, "expert", split_axis=0, concat_axis=0, tiled=True),
        lax.all_to_all(fan_p, "expert", split_axis=0, concat_axis=0, tiled=True),
    )
    xs = got[0].reshape(total_rows, width)
    dys = got[1].reshape(total_rows, width)
    weights = got[2].reshape(total_rows)
    dx_part, score, grad_gu, grad_out = expert_side(xs, dys, weights, w_gate_up, w_down)
    back = (
        lax.all_to_all(
            dx_part.astype(jnp.bfloat16).reshape(columns, groups, capacity, width),
            "expert",
            split_axis=0,
            concat_axis=0,
            tiled=True,
        ),
        lax.all_to_all(
            score.astype(jnp.bfloat16).reshape(columns, groups, capacity),
            "expert",
            split_axis=0,
            concat_axis=0,
            tiled=True,
        ),
    )
    dx_sum = jnp.sum(
        back[0].reshape(4, slices, groups, capacity, width).astype(jnp.float32), axis=1
    ).astype(jnp.bfloat16)
    score_sum = jnp.sum(
        back[1].reshape(4, slices, groups, capacity).astype(jnp.float32), axis=1
    ).astype(jnp.bfloat16)
    home = (
        lax.all_to_all(dx_sum, "seq", split_axis=1, concat_axis=0, tiled=True),
        lax.all_to_all(score_sum, "seq", split_axis=1, concat_axis=0, tiled=True),
    )
    slot_dx = home[0].reshape(experts * capacity, width)
    slot_score = home[1].reshape(experts * capacity)
    grad_tokens = lax.dot_general(
        token_pick, slot_dx, (((0,), (0,)), ((), ())), preferred_element_type=jnp.float32
    ).astype(jnp.bfloat16)
    grad_probs = jnp.sum(pick_float * slot_score.astype(jnp.float32)[:, None], axis=0).reshape(
        rows, top
    )
    return (grad_tokens, grad_probs, grad_gu, grad_out)


def solution(mesh):
    in_specs = (
        P(("seq", "expert"), None),
        P(("seq", "expert"), None),
        P(("seq", "expert"), None),
        P(("seq", "expert"), None),
        P(("seq", "expert"), None, None, None),
        P(("seq", "expert"), None, None),
    )
    out_specs = (
        P(("seq", "expert"), None),
        P(("seq", "expert"), None),
        P(("seq", "expert"), None, None, None),
        P(("seq", "expert"), None, None),
    )
    return jax.shard_map(body, mesh=mesh, in_specs=in_specs, out_specs=out_specs, check_vma=False)
```

profile of v0, /device:TPU:2, one launch (start us, length us, event | category | flops | bytes accessed | tf_op | source)
XLA Modules:
  0.0 747.5 jit_solution(9181529959032977705)
XLA Ops:
  0.6 0.8 copy.74
  2.1 0.7 multiply_add_fusion
  2.9 2.0 fusion.7
  4.9 9.3 %all-to-all-start.4 = ((bf16[16,8,2048]{2,1,0:T(8,128)(2,1)}), bf16[16,8,2048]{2,1,0:T(8,128)(2,1)S(1)}, u32[]{:S(2)}, u32[]{:S(2)}) async-start(bf16[16,8,2048]{2,1,0:T(8,128)(2,1)} %fusion.7), calls=%async_computation.4 | async-start | bytes 1048576 | tf_op jit(solution)/shard_map/all_to_all | solution.py:68
  14.2 2.0 fusion.6
  16.2 6.8 all-to-all-done.4
  23.0 4.9 all-to-all-start.2
  27.9 0.3 reshape.129
  28.2 0.4 copy.82
  28.6 8.1 %all-to-all-done.2 = bf16[16,8,2048]{2,1,0:T(8,128)(2,1)S(1)} async-done(((bf16[16,8,2048]{2,1,0:T(8,128)(2,1)}), bf16[16,8,2048]{2,1,0:T(8,128)(2,1)S(1)}, u32[]{:S(2)}, u32[]{:S(2)}) %all-to-all-start.2) | async-done | bytes 524320 | tf_op jit(solution)/shard_map/all_to_all | solution.py:75
  36.7 5.7 broadcast_in_dim.22
  42.5 15.5 %all-to-all-start.5 = ((bf16[32,16,2,2048]{3,2,1,0:T(2,128)(2,1)}), bf16[32,16,2,2048]{3,2,1,0:T(2,128)(2,1)}, u32[]{:S(2)}, u32[]{:S(2)}) async-start(bf16[32,16,2,2048]{3,2,1,0:T(2,128)(2,1)} %bitcast.66), calls=%async_computation.5 | async-start | bytes 8388608 | tf_op jit(solution)/shard_map/all_to_all | solution.py:93
  58.0 0.3 reshape.125
  58.4 0.4 copy.81
  58.8 182.7 %all-to-all-done.5 = bf16[32,16,2,2048]{3,2,1,0:T(2,128)(2,1)} async-done(((bf16[32,16,2,2048]{3,2,1,0:T(2,128)(2,1)}), bf16[32,16,2,2048]{3,2,1,0:T(2,128)(2,1)}, u32[]{:S(2)}, u32[]{:S(2)}) %all-to-all-start.5) | async-done | bytes 4194336 | tf_op jit(solution)/shard_map/all_to_all | solution.py:93
  241.5 5.7 broadcast_in_dim.21
  247.3 10.4 %all-to-all-start.3 = ((bf16[32,16,2,2048]{3,2,1,0:T(2,128)(2,1)}), bf16[32,16,2,2048]{3,2,1,0:T(2,128)(2,1)}, u32[]{:S(2)}, u32[]{:S(2)}) async-start(bf16[32,16,2,2048]{3,2,1,0:T(2,128)(2,1)} %bitcast.67), calls=%async_computation.3 | async-start | bytes 8388608 | tf_op jit(solution)/shard_map/all_to_all | solution.py:94
  257.7 7.3 reshape.131
  265.0 3.9 fusion.10
  268.9 2.5 fusion.13
  271.4 169.9 %all-to-all-done.3 = bf16[32,16,2,2048]{3,2,1,0:T(2,128)(2,1)} async-done(((bf16[32,16,2,2048]{3,2,1,0:T(2,128)(2,1)}), bf16[32,16,2,2048]{3,2,1,0:T(2,128)(2,1)}, u32[]{:S(2)}, u32[]{:S(2)}) %all-to-all-start.3) | async-done | bytes 4194336 | tf_op jit(solution)/shard_map/all_to_all | solution.py:94
  441.3 7.2 reshape.127
  448.5 4.8 multiply_reduce_fusion
  453.3 0.3 convert_element_type.117
  453.6 0.2 copy.84
  453.8 22.1 %all_to_all.65 = bf16[32,16,2]{1,2,0:T(2,128)(2,1)S(1)} all-to-all(bf16[32,16,2]{1,2,0:T(2,128)(2,1)S(1)} %copy.84), channel_id=1, replica_groups=mesh['seq'=16,'expert'=32] {'expert'}, dimensions={0} | all-to-all | bytes 4096 | tf_op jit(solution)/shard_map/all_to_all | solution.py:109
  476.0 0.7 copy.86
  476.7 4.7 all-to-all-start.9
  481.6 6.0 all-to-all-done.9
  488.2 10.6 %all_to_all.66 = bf16[16,1,8]{2,1,0:T(2,128)(2,1)S(1)} all-to-all(bf16[16,1,8]{2,1,0:T(2,128)(2,1)S(1)} %convert_element_type.133), channel_id=1, replica_groups=mesh['seq'=16,'expert'=32] {'seq'}, dimensions={0} | all-to-all | bytes 512 | tf_op jit(solution)/shard_map/all_to_all | solution.py:82
  498.9 15.4 %all_to_all.67 = bf16[32,16,2]{1,2,0:T(2,128)(2,1)S(1)} all-to-all(bf16[32,16,2]{1,2,0:T(2,128)(2,1)S(1)} %bitcast.71), channel_id=1, replica_groups=mesh['seq'=16,'expert'=32] {'expert'}, dimensions={0} | all-to-all | bytes 4096 | tf_op jit(solution)/shard_map/all_to_all | solution.py:95
  514.4 0.2 copy.80
  514.7 1.9 multiply_convert_fusion.6
  516.6 1.3 fusion.8
  517.9 3.3 add_convert_fusion
  521.2 7.7 %reshape.132 = bf16[32,16,2,2048]{3,2,1,0:T(2,128)(2,1)} reshape(bf16[1024,2048]{1,0:T(8,128)(2,1)} %add_convert_fusion) | data formatting | bytes 8388608 | tf_op jit(solution)/shard_map/reshape | solution.py:103
  528.9 5.1 all-to-all-start.6
  534.1 0.7 copy.89
  534.7 3.3 fusion.5
  538.2 1.0 fusion.4
  539.2 1.2 maximum_bitcast_fusion
  540.4 184.7 %all-to-all-done.6 = bf16[32,16,2,2048]{3,2,1,0:T(2,128)(2,1)} async-done(((bf16[32,16,2,2048]{3,2,1,0:T(2,128)(2,1)}), bf16[32,16,2,2048]{3,2,1,0:T(2,128)(2,1)}, u32[]{:S(2)}, u32[]{:S(2)}) %all-to-all-start.6) | async-done | bytes 4194336 | tf_op jit(solution)/shard_map/all_to_all | solution.py:102
  725.1 6.4 bitcast_reduce_fusion
  731.5 1.3 copy.83
  732.8 4.8 all-to-all-start.7
  737.7 4.2 fusion.3
  741.9 4.6 all-to-all-done.7
  746.7 0.8 convolution_convert_fusion.4
  (39 shorter events, 2.4 us)
Async XLA Ops:
  0.6 447.8 %copy-start = (bf16[1,176,2048]{2,1,0:T(8,128)(2,1)S(1)}, bf16[1,176,2048]{2,1,0:T(8,128)(2,1)}, u32[]{:S(2)}) copy-start(bf16[1,176,2048]{2,1,0:T(8,128)(2,1)} %param.11) | copy-start | bytes 2162692
  4.9 18.1 %all-to-all-start.4 = ((bf16[16,8,2048]{2,1,0:T(8,128)(2,1)}), bf16[16,8,2048]{2,1,0:T(8,128)(2,1)S(1)}, u32[]{:S(2)}, u32[]{:S(2)}) async-start(bf16[16,8,2048]{2,1,0:T(8,128)(2,1)} %fusion.7), calls=%async_computation.4 | async-start | bytes 1048576 | tf_op jit(solution)/shard_map/all_to_all | solution.py:68
  23.0 13.7 %all-to-all-start.2 = ((bf16[16,8,2048]{2,1,0:T(8,128)(2,1)}), bf16[16,8,2048]{2,1,0:T(8,128)(2,1)S(1)}, u32[]{:S(2)}, u32[]{:S(2)}) async-start(bf16[16,8,2048]{2,1,0:T(8,128)(2,1)} %fusion.6), calls=%async_computation.2 | async-start | bytes 1048576 | tf_op jit(solution)/shard_map/all_to_all | solution.py:75
  42.5 199.0 %all-to-all-start.5 = ((bf16[32,16,2,2048]{3,2,1,0:T(2,128)(2,1)}), bf16[32,16,2,2048]{3,2,1,0:T(2,128)(2,1)}, u32[]{:S(2)}, u32[]{:S(2)}) async-start(bf16[32,16,2,2048]{3,2,1,0:T(2,128)(2,1)} %bitcast.66), calls=%async_computation.5 | async-start | bytes 8388608 | tf_op jit(solution)/shard_map/all_to_all | solution.py:93
  247.3 194.0 %all-to-all-start.3 = ((bf16[32,16,2,2048]{3,2,1,0:T(2,128)(2,1)}), bf16[32,16,2,2048]{3,2,1,0:T(2,128)(2,1)}, u32[]{:S(2)}, u32[]{:S(2)}) async-start(bf16[32,16,2,2048]{3,2,1,0:T(2,128)(2,1)} %bitcast.67), calls=%async_computation.3 | async-start | bytes 8388608 | tf_op jit(solution)/shard_map/all_to_all | solution.py:94
  257.7 7.3 copy-start.3
  265.0 3.9 copy-start.1
  268.9 179.6 %copy-start.4 = (f32[1024,176]{0,1:T(8,128)}, f32[1024,176]{0,1:T(8,128)S(1)}, u32[]{:S(2)}) copy-start(f32[1024,176]{0,1:T(8,128)S(1)} %fusion.10) | copy-start | bytes 2162692
  448.5 32.9 %copy-start.7 = (bf16[16,6]{0,1:T(8,128)(2,1)S(1)}, bf16[16,6]{0,1:T(8,128)(2,1)}, u32[]{:S(2)}) copy-start(bf16[16,6]{0,1:T(8,128)(2,1)} %param.9) | copy-start | bytes 580
  476.7 10.9 %all-to-all-start.9 = ((bf16[4,16,2]{0,2,1:T(2,128)(2,1)}), bf16[4,16,2]{0,2,1:T(2,128)(2,1)S(1)}, u32[]{:S(2)}, u32[]{:S(2)}) async-start(bf16[4,16,2]{0,2,1:T(2,128)(2,1)} %copy.86), calls=%async_computation.9 | async-start | bytes 16384 | tf_op jit(solution)/shard_map/all_to_all | solution.py:125
  528.9 196.2 %all-to-all-start.6 = ((bf16[32,16,2,2048]{3,2,1,0:T(2,128)(2,1)}), bf16[32,16,2,2048]{3,2,1,0:T(2,128)(2,1)}, u32[]{:S(2)}, u32[]{:S(2)}) async-start(bf16[32,16,2,2048]{3,2,1,0:T(2,128)(2,1)} %reshape.132), calls=%async_computation.6 | async-start | bytes 8388608 | tf_op jit(solution)/shard_map/all_to_all | solution.py:102
  534.7 3.4 copy-start.2
  539.2 198.5 %copy-start.5 = (f32[1024,176]{0,1:T(8,128)S(1)}, f32[1024,176]{0,1:T(8,128)}, u32[]{:S(2)}) copy-start(f32[1024,176]{0,1:T(8,128)} %copy-done.4) | copy-start | bytes 2162692
  539.2 198.5 %copy-start.6 = (f32[1024,176]{0,1:T(8,128)S(1)}, f32[1024,176]{0,1:T(8,128)}, u32[]{:S(2)}) copy-start(f32[1024,176]{0,1:T(8,128)} %fusion.13) | copy-start | bytes 2162692
  732.8 13.7 %all-to-all-start.7 = ((bf16[4,16,2,2048]{3,2,0,1:T(2,128)(2,1)}), bf16[4,16,2,2048]{3,2,0,1:T(2,128)(2,1)S(1)}, u32[]{:S(2)}, u32[]{:S(2)}) async-start(bf16[4,16,2,2048]{3,2,0,1:T(2,128)(2,1)} %copy.83), calls=%async_computation.7 | async-start | bytes 1048576 | tf_op jit(solution)/shard_map/all_to_all | solution.py:124
where the time goes:
time: 749 us; the launch traced here: 748 us
  waiting for transfers between devices  563 us (75%)
  starting transfers between devices  54.7 us (7%)
  blocking collectives  48.1 us (6%)
  local copies, waits for them, and re-layouts  41.1 us (5%)
  matrix products  28.9 us (4%)
  other arithmetic  11 us (1%)
    all_to_all x1, waiting for transfers between devices, body(): lax.all_to_all(dx_part.astype(jnp.bfloat16).reshape(columns, groups, capa...  185 us
    all_to_all x1, waiting for transfers between devices, body(): lax.all_to_all(fan_x, 'expert', split_axis=0, concat_axis=0, tiled=True)  183 us
    all_to_all x1, waiting for transfers between devices, body(): lax.all_to_all(fan_dy, 'expert', split_axis=0, concat_axis=0, tiled=True)  170 us
    all_to_all x1, blocking collectives, body(): lax.all_to_all(score.astype(jnp.bfloat16).reshape(columns, groups, capaci...  22.1 us
    all_to_all x1, starting transfers between devices, body(): lax.all_to_all(fan_x, 'expert', split_axis=0, concat_axis=0, tiled=True)  15.5 us
    all_to_all x1, blocking collectives, body(): lax.all_to_all(fan_p, 'expert', split_axis=0, concat_axis=0, tiled=True)  15.4 us
  transfers between devices with their start and end apart: 7, of which 7 were waited for; matrix products, arithmetic and copies ran while one was open for 4% of the time, Pallas kernels for 0%

commit v1 on v0

v1 whole, which is shorter than its diff:
```python
import functools

import jax
import jax.numpy as jnp
from jax import lax
from jax.experimental import pallas as pl
from jax.experimental.pallas import tpu as pltpu
from jax.sharding import PartitionSpec as P

MESH = pl.DeviceIdType.MESH
CAP = 2
EXTRA = 128
BF = jnp.bfloat16
F32 = jnp.float32


def dot(a, b, ca, cb):
    return lax.dot_general(a, b, (((ca,), (cb,)), ((), ())), preferred_element_type=F32)


def tiles(width, size):
    return [(at, min(size, width - at)) for at in range(0, width, size)]


def kernel(
    G,
    Z,
    top,
    tok_ref,
    og_ref,
    meta_ref,
    wgu_hbm,
    wd_hbm,
    gt_ref,
    gp_ref,
    ggu_hbm,
    gd_hbm,
    xm,
    dyb,
    sbuf,
    rbuf,
    pt,
    wgu,
    wd,
    ggt,
    actt,
    dxo,
    dxs,
    dxr,
    rts,
    rtr,
    tp,
    rss,
    rsr,
    ggu,
    gd,
    ag_send,
    ag_recv,
    ip_send,
    ip_recv,
    sw_send,
    sw_recv,
    dx_send,
    dx_recv,
    rt_send,
    rt_recv,
    rs_send,
    rs_recv,
    w_sem,
    o_sem,
):
    B, D = tok_ref.shape
    H = wd.shape[0]
    W2 = D + EXTRA
    half = Z // 2
    quarter = Z // 4
    R = half * CAP
    rows = G * R
    nt = half * B
    side = 4 if G == 16 else 0

    s = lax.axis_index("seq")
    e = lax.axis_index("expert")
    z = e // 2
    c = e % 2
    q = e // (Z * 2 // 4)
    expert = s * 4 + q
    right = lax.rem(z + 1, Z) * 2 + c
    left = lax.rem(z + Z - 1, Z) * 2 + c
    partner = z * 2 + 1 - c

    def ahead(i):
        if side:
            return lax.rem(s // side + i // side, side) * side + lax.rem(s % side + i % side, side)
        return lax.rem(s + i, G)

    def behind(i):
        if side:
            return lax.rem(s // side + side - i // side, side) * side + lax.rem(
                s % side + side - i % side, side
            )
        return lax.rem(s + G - i, G)

    def loop(lo, hi, fn):
        def step(i, carry):
            fn(i)
            return carry

        lax.fori_loop(lo, hi, step, 0)

    w_copies = [
        pltpu.make_async_copy(wgu_hbm.at[0], wgu, w_sem.at[0]),
        pltpu.make_async_copy(wd_hbm.at[0], wd, w_sem.at[1]),
    ]
    for copy in w_copies:
        copy.start()

    barrier = pltpu.get_barrier_semaphore()

    def greet(i):
        pl.semaphore_signal(barrier, inc=1, device_id=(ahead(i), e), device_id_type=MESH)

    loop(1, G, greet)
    for other in (right, left, partner):
        pl.semaphore_signal(barrier, inc=1, device_id=(s, other), device_id_type=MESH)

    def pos(rel):
        return lax.rem(rel + quarter + 2 * Z, Z)

    own = quarter
    xm[own, :, :D] = tok_ref[...]
    xm[own, :, D:] = meta_ref[...]
    dyb[own] = og_ref[...]

    pl.semaphore_wait(barrier, G - 1 + 3)

    def ag(way, i, piece):
        buf = xm if piece == 0 else dyb
        src, dst = (pos(-i), pos(-i - 1)) if way == 0 else (pos(i), pos(i + 1))
        return pltpu.make_async_remote_copy(
            src_ref=buf.at[src],
            dst_ref=buf.at[dst],
            send_sem=ag_send.at[way, piece, i],
            recv_sem=ag_recv.at[way, piece, i],
            device_id=(s, right if way == 0 else left),
            device_id_type=MESH,
        )

    def ag_step(i):
        for piece in range(2):
            for way in range(2):
                ag(way, i - 1, piece).wait_recv()
                ag(way, i, piece).start()

    def ag_last():
        for piece in range(2):
            for way in range(2):
                ag(way, half - 2, piece).wait_recv()
            ag(0, half - 1, piece).start()

    def ip(ch, piece, to, frm):
        return pltpu.make_async_remote_copy(
            src_ref=sbuf.at[ch, piece, pl.ds(to * R, R)],
            dst_ref=rbuf.at[c, ch, piece, pl.ds(frm * R, R)],
            send_sem=ip_send.at[ch, piece, to],
            recv_sem=ip_recv.at[ch, piece, frm],
            device_id=(to, e),
            device_id_type=MESH,
        )

    def ip_own(ch, piece):
        return pltpu.make_async_copy(
            sbuf.at[ch, piece, pl.ds(s * R, R)],
            rbuf.at[c, ch, piece, pl.ds(s * R, R)],
            ip_send.at[ch, piece, s],
        )

    def iota(shape, dim):
        return lax.broadcasted_iota(jnp.int32, shape, dim)

    def log2(n):
        return n.bit_length() - 1

    def pick(ch):
        blocks = pl.ds(ch * half, half)
        meta = xm[blocks, :, D:].reshape(nt, EXTRA).astype(F32)
        lane_expert = (iota((nt, EXTRA), 1) * 4 + q).astype(F32)
        member = jnp.zeros((nt, EXTRA), F32)
        weight = jnp.zeros((nt, EXTRA), F32)
        for k in range(top):
            hit = jnp.broadcast_to(meta[:, k : k + 1], (nt, EXTRA)) == lane_expert
            member = member + jnp.where(hit, 1.0, 0.0)
            weight = weight + jnp.where(
                hit, jnp.broadcast_to(meta[:, 8 + k : 9 + k], (nt, EXTRA)), 0.0
            )
        member = member.astype(BF)
        weight = weight.astype(BF)
        ti, tj = iota((nt, nt), 0), iota((nt, nt), 1)
        earlier = ((ti >> log2(B)) == (tj >> log2(B))) & (tj < ti)
        rank = dot(jnp.where(earlier, 1.0, 0.0).astype(BF), member, 1, 0).astype(BF)
        spread = jnp.where(
            iota((EXTRA, rows), 0) == (iota((EXTRA, rows), 1) >> log2(R)), 1.0, 0.0
        ).astype(BF)
        member_s = dot(member, spread, 1, 0)
        rank_s = dot(rank, spread, 1, 0)
        weight_s = dot(weight, spread, 1, 0)
        tok, slot = iota((nt, rows), 0), iota((nt, rows), 1)
        mine = (tok >> log2(B)) == ((slot & (R - 1)) >> 1)
        chosen = (member_s > 0.5) & (rank_s == (slot & 1).astype(F32)) & mine
        picked = jnp.where(chosen, 1.0, 0.0).astype(BF)
        pt[ch] = picked
        for piece in range(2):
            matrix = picked if piece == 0 else jnp.where(chosen, weight_s, 0.0).astype(BF)
            for at, wide in tiles(D, 512):
                if piece == 0:
                    block = xm[blocks, :, at : at + wide].reshape(nt, wide)
                else:
                    block = dyb[blocks, :, at : at + wide].reshape(nt, wide)
                sbuf[ch, piece, :, at : at + wide] = dot(matrix, block, 0, 0).astype(BF)
            loop(1, G, lambda i: ip(ch, piece, ahead(i), s).start())
            ip_own(ch, piece).start()

    for piece in range(2):
        for way in range(2):
            ag(way, 0, piece).start()
    if quarter < half - 1:
        loop(1, quarter + 1, ag_step)
        pick(0)
        loop(quarter + 1, half - 1, ag_step)
        ag_last()
    else:
        loop(1, half - 1, ag_step)
        ag_last()
        pick(0)
    for piece in range(2):
        ag(0, half - 1, piece).wait_recv()
    pick(1)

    def sw(ch, piece, frm, core):
        return pltpu.make_async_remote_copy(
            src_ref=rbuf.at[core, ch, piece, pl.ds(frm * R, R)],
            dst_ref=rbuf.at[core, ch, piece, pl.ds(frm * R, R)],
            send_sem=sw_send.at[ch, piece, frm],
            recv_sem=sw_recv.at[ch, piece, frm],
            device_id=(s, partner),
            device_id_type=MESH,
        )

    def swap(ch, piece):
        ip_own(ch, piece).wait()
        sw(ch, piece, s, c).start()

        def forward(i):
            frm = behind(i)
            ip(ch, piece, frm, frm).wait_recv()
            sw(ch, piece, frm, c).start()

        loop(1, G, forward)

    def swapped(ch, piece):
        loop(0, G, lambda i: sw(ch, piece, i, 1 - c).wait_recv())

    def forward_part(ch, core, unit):
        x = rbuf[core, ch, 0]
        gu = dot(wgu[...].reshape(2 * H, D), x, 1, 1)
        gate, upper = gu[:H], gu[H:]
        err = dot(wd[...], rbuf[core, ch, 1], 1, 1)
        sig = jax.nn.sigmoid(gate)
        act = gate * sig * upper
        actt[unit] = act.astype(BF)
        ggt[unit, :H] = (err * upper * sig * (1.0 + gate * (1.0 - sig))).astype(BF)
        ggt[unit, H:] = (err * gate * sig).astype(BF)
        score = jnp.sum(err * act, axis=0, keepdims=True)
        score = jnp.broadcast_to(score, (16, rows)).astype(BF)
        mark = (iota((16, EXTRA), 0) == 0) & (iota((16, EXTRA), 1) == expert)
        return dot(score, jnp.where(mark, 1.0, 0.0).astype(BF), 0, 0)

    def dx_part(unit, put):
        for at, wide in tiles(D, 512):
            w = wgu[:, :, at : at + wide].reshape(2 * H, wide)
            put(at, wide, dot(ggt[unit], w, 0, 0))

    def dx_copy(ch):
        return pltpu.make_async_remote_copy(
            src_ref=dxs.at[ch],
            dst_ref=dxr.at[ch],
            send_sem=dx_send.at[ch],
            recv_sem=dx_recv.at[ch],
            device_id=(s, partner),
            device_id_type=MESH,
        )

    def rt(ch, to, frm):
        return pltpu.make_async_remote_copy(
            src_ref=rts.at[ch, pl.ds(to * R, R)],
            dst_ref=rtr.at[ch, pl.ds(frm * R, R)],
            send_sem=rt_send.at[ch, to],
            recv_sem=rt_recv.at[ch, frm],
            device_id=(to, e),
            device_id_type=MESH,
        )

    def rt_own(ch):
        return pltpu.make_async_copy(
            rts.at[ch, pl.ds(s * R, R)], rtr.at[ch, pl.ds(s * R, R)], rt_send.at[ch, s]
        )

    def compute(ch):
        def put_other(at, wide, value):
            dxs[ch, :, at : at + wide] = value.astype(BF)

        def put_own(at, wide, value):
            dxo[:, at : at + wide] = value

        put_other(D, EXTRA, forward_part(ch, 1 - c, 2 * ch))
        dx_part(2 * ch, put_other)
        dx_copy(ch).start()
        put_own(D, EXTRA, forward_part(ch, c, 2 * ch + 1))
        dx_part(2 * ch + 1, put_own)
        dx_copy(ch).wait_recv()
        for at, wide in tiles(W2, 512):
            cols = slice(at, at + wide)
            rts[ch, :, cols] = (dxo[:, cols] + dxr[ch, :, cols].astype(F32)).astype(BF)
        loop(1, G, lambda i: rt(ch, ahead(i), s).start())
        rt_own(ch).start()

    for piece in range(2):
        swap(0, piece)
    for copy in w_copies:
        copy.wait()
    for piece in range(2):
        swapped(0, piece)
    compute(0)
    for piece in range(2):
        swap(1, piece)
    for piece in range(2):
        swapped(1, piece)
    compute(1)

    for at, wide in tiles(D, 512):
        cols = slice(at, at + wide)
        total = jnp.zeros((2 * H, wide), F32)
        total_down = jnp.zeros((H, wide), F32)
        for unit in range(4):
            core = (1 - c) if unit % 2 == 0 else c
            total = total + dot(ggt[unit], rbuf[core, unit // 2, 0, :, cols], 1, 0)
            total_down = total_down + dot(actt[unit], rbuf[core, unit // 2, 1, :, cols], 1, 0)
        ggu[:, :, cols] = total.astype(BF).reshape(2, H, wide)
        gd[:, cols] = total_down.astype(BF)
    o_copies = [
        pltpu.make_async_copy(ggu, ggu_hbm.at[0], o_sem.at[0]),
        pltpu.make_async_copy(gd, gd_hbm.at[0], o_sem.at[1]),
    ]
    for copy in o_copies:
        copy.start()

    for ch in range(2):
        rt_own(ch).wait()

        def back(i):
            frm = behind(i)
            rt(ch, frm, frm).wait_recv()

        loop(1, G, back)
        for at, wide in tiles(W2, 512):
            value = dot(pt[ch], rtr[ch, :, at : at + wide], 1, 0)
            tp[ch * half : (ch + 1) * half, :, at : at + wide] = value.reshape(half, B, wide)

    def rs(way, i):
        return pltpu.make_async_remote_copy(
            src_ref=rss.at[way, i],
            dst_ref=rsr.at[way, i],
            send_sem=rs_send.at[way, i],
            recv_sem=rs_recv.at[way, i],
            device_id=(s, right if way == 0 else left),
            device_id_type=MESH,
        )

    def rs_rel(way, i):
        return half - i if way == 0 else -(half - 1 - i)

    for way in range(2):
        rss[way, 0] = tp[pos(rs_rel(way, 0))].astype(BF)
        rs(way, 0).start()

    def rs_step(i, ways=(0, 1)):
        for way in ways:
            rs(way, i - 1).wait_recv()
            rss[way, i] = (tp[pos(rs_rel(way, i))] + rsr[way, i - 1].astype(F32)).astype(BF)
            rs(way, i).start()

    loop(1, half - 1, rs_step)
    rs_step(half - 1, (0,))
    rs(1, half - 2).wait_recv()
    rs(0, half - 1).wait_recv()
    total = tp[own] + rsr[0, half - 1].astype(F32) + rsr[1, half - 2].astype(F32)
    gt_ref[...] = total[:, :D].astype(BF)
    scores = total[:, D:]
    meta = meta_ref[...].astype(F32)
    lane = iota((B, EXTRA), 1).astype(F32)
    for k in range(top):
        hit = jnp.broadcast_to(meta[:, k : k + 1], (B, EXTRA)) == lane
        value = jnp.sum(jnp.where(hit, scores, 0.0), axis=1, keepdims=True)
        gp_ref[:, k : k + 1] = value / meta[:, 8 + k : 9 + k]

    for piece in range(2):
        loop(0, half - 1, lambda i: ag(0, i, piece).wait_send())
        loop(0, half - 1, lambda i: ag(1, i, piece).wait_send())
        ag(0, half - 1, piece).wait_send()
    for ch in range(2):
        for piece in range(2):
            loop(1, G, lambda i: ip(ch, piece, ahead(i), s).wait_send())
            loop(0, G, lambda i: sw(ch, piece, i, c).wait_send())
        dx_copy(ch).wait_send()
        loop(1, G, lambda i: rt(ch, ahead(i), s).wait_send())
    loop(0, half - 1, lambda i: rs(0, i).wait_send())
    loop(0, half - 1, lambda i: rs(1, i).wait_send())
    rs(0, half - 1).wait_send()
    for copy in o_copies:
        copy.wait()


def body(tokens, out_grads, route_ids, route_probs, w_gate_up, w_down):
    B, D = tokens.shape
    top = route_ids.shape[1]
    H = w_down.shape[1]
    G = lax.axis_size("seq")
    Z = lax.axis_size("expert") // 2
    half = Z // 2
    R = half * CAP
    rows = G * R
    nt = half * B
    W2 = D + EXTRA
    meta = jnp.concatenate(
        [
            route_ids.astype(BF),
            jnp.zeros((B, 8 - top), BF),
            route_probs,
            jnp.zeros((B, EXTRA - 8 - top), BF),
        ],
        axis=1,
    )
    vmem = pl.BlockSpec(memory_space=pltpu.VMEM)
    anys = pl.BlockSpec(memory_space=pl.ANY)
    dma = pltpu.SemaphoreType.DMA
    gt, gp, ggu, gd = pl.pallas_call(
        functools.partial(kernel, G, Z, top),
        out_shape=(
            jax.ShapeDtypeStruct((B, D), BF),
            jax.ShapeDtypeStruct((B, top), F32),
            jax.ShapeDtypeStruct(w_gate_up.shape, BF),
            jax.ShapeDtypeStruct(w_down.shape, BF),
        ),
        in_specs=[vmem, vmem, vmem, anys, anys],
        out_specs=(vmem, vmem, anys, anys),
        scratch_shapes=[
            pltpu.VMEM((Z, B, W2), BF),
            pltpu.VMEM((Z, B, D), BF),
            pltpu.VMEM((2, 2, rows, D), BF),
            pltpu.VMEM((2, 2, 2, rows, D), BF),
            pltpu.VMEM((2, nt, rows), BF),
            pltpu.VMEM((2, H, D), BF),
            pltpu.VMEM((H, D), BF),
            pltpu.VMEM((4, 2 * H, rows), BF),
            pltpu.VMEM((4, H, rows), BF),
            pltpu.VMEM((rows, W2), F32),
            pltpu.VMEM((2, rows, W2), BF),
            pltpu.VMEM((2, rows, W2), BF),
            pltpu.VMEM((2, rows, W2), BF),
            pltpu.VMEM((2, rows, W2), BF),
            pltpu.VMEM((Z, B, W2), F32),
            pltpu.VMEM((2, half, B, W2), BF),
            pltpu.VMEM((2, half, B, W2), BF),
            pltpu.VMEM((2, H, D), BF),
            pltpu.VMEM((H, D), BF),
            dma((2, 2, half)),
            dma((2, 2, half)),
            dma((2, 2, G)),
            dma((2, 2, G)),
            dma((2, 2, G)),
            dma((2, 2, G)),
            dma((2,)),
            dma((2,)),
            dma((2, G)),
            dma((2, G)),
            dma((2, half)),
            dma((2, half)),
            dma((2,)),
            dma((2,)),
        ],
        compiler_params=pltpu.CompilerParams(
            collective_id=0, has_side_effects=True, vmem_limit_bytes=56 * 1024 * 1024
        ),
        name="moe_backward",
    )(tokens, out_grads, meta, w_gate_up, w_down)
    return gt, gp, ggu, gd


def solution(mesh):
    in_specs = (
        P(("seq", "expert"), None),
        P(("seq", "expert"), None),
        P(("seq", "expert"), None),
        P(("seq", "expert"), None),
        P(("seq", "expert"), None, None, None),
        P(("seq", "expert"), None, None),
    )
    out_specs = (
        P(("seq", "expert"), None),
        P(("seq", "expert"), None),
        P(("seq", "expert"), None, None, None),
        P(("seq", "expert"), None, None),
    )
    return jax.shard_map(body, mesh=mesh, in_specs=in_specs, out_specs=out_specs, check_vma=False)
```

time: 749 us -> 154 us (0.21)
  the two profiles are of different devices: /device:TPU:2 before, /device:TPU:20 now
where the time goes in v1:
time: 154 us; the launch traced here: 153 us
  Pallas kernels  144 us (94%)
  local copies, waits for them, and re-layouts  7.42 us (5%)
    pallas_call x1, Pallas kernels, body(): pl.pallas_call(functools.partial(kernel, G, Z, top), out_shape=(jax.Shape...  144 us
    unnamed x6, local copies, waits for them, and re-layouts  5.8 us

profile of v1, /device:TPU:20, one launch (start us, length us, event | category | flops | bytes accessed | tf_op | source)
XLA Modules:
  0.0 153.2 jit_solution(10679359993816955979)
XLA Ops:
  0.6 0.1 pad.3.clone
  0.7 0.1 pad.1.clone
  0.8 0.7 convert_element_type.3
  1.5 0.1 copy.13
  1.6 0.8 copy.14
  2.4 0.7 maximum_maximum_fusion.meta_ref
  3.0 143.7 %moe_backward.1 = (bf16[16,2048]{1,0:T(8,128)(2,1)}, f32[16,6]{1,0:T(8,128)}, bf16[1,2,176,2048]{3,2,1,0:T(8,128)(2,1)}, bf16[1,176,2048]{2,1,0:T(8,128)(2,1)}) custom-call(bf16[16,2048]{1,0:T(8,128)(2,1)} %tok_ref.1, bf16[16,2048]{1,0:T(8,128)(2,1)} %og_ref.1, bf16[16,128]{1,0:T(8,128)(2,1)} %maximum_maximum_fusion.meta_ref, ...), custom_call_target="tpu_custom_call" | custom-call | tf_op jit(solution)/shard_map/moe_backward/pallas_call | solution.py:446
  146.8 1.4 copy.15
  148.1 1.5 copy.19
  149.6 0.0 copy-start
  149.6 2.7 %copy.20 = bf16[1,2,176,2048]{3,2,1,0:T(8,128)(2,1)} copy(bf16[1,2,176,2048]{3,2,1,0:T(8,128)(2,1)} %get-tuple-element.18) | data formatting | bytes 2883584
  152.3 0.0 copy-done
  152.3 0.9 copy.21
  (2 shorter events, 0.0 us)
Async XLA Ops:
  149.6 2.7 %copy-start = (bf16[1,176,2048]{2,1,0:T(8,128)(2,1)S(1)}, bf16[1,176,2048]{2,1,0:T(8,128)(2,1)}, u32[]{:S(2)}) copy-start(bf16[1,176,2048]{2,1,0:T(8,128)(2,1)} %get-tuple-element.19) | copy-start | bytes 2162692

commit v2 on v1

v2 whole, which is shorter than its diff:
```python
import functools

import jax
import jax.numpy as jnp
from jax import lax
from jax.experimental import pallas as pl
from jax.experimental.pallas import tpu as pltpu
from jax.sharding import PartitionSpec as P

MESH = pl.DeviceIdType.MESH
CAP = 2
EXTRA = 128
BF = jnp.bfloat16
F32 = jnp.float32


def dot(a, b, ca, cb):
    return lax.dot_general(a, b, (((ca,), (cb,)), ((), ())), preferred_element_type=F32)


def tiles(width, size):
    return [(at, min(size, width - at)) for at in range(0, width, size)]


BLOCKS = (-2, -1, 0, 1, -4, -3, 2, 3, -6, -5, 4, 5, -8, -7, 6, 7)
POS = {rel: at for at, rel in enumerate(BLOCKS)}
NEAR = (-4, 3, -3, 2, -2, 1, -1)
FAR = ((1, 6, 0), (2, 7, 0), (-1, 4, 0), (1, -5, 1), (-1, -7, 1), (-2, -8, 1))
LAST = ((5, 5), (-6, -6))
GREET = (-3, -2, -1, 1, 2, 3, 4, -5, 6)


def kernel(
    G,
    Z,
    top,
    pieces,
    tok_ref,
    og_ref,
    ids_ref,
    probs_ref,
    wgu_hbm,
    wd_hbm,
    gt_ref,
    gp_ref,
    ggu_hbm,
    gd_hbm,
    xm,
    dyb,
    sbuf,
    rbuf,
    pt,
    wgu,
    wd,
    ggt,
    actt,
    rts,
    rtr,
    tp,
    nrs,
    nrr,
    frs,
    frr,
    lrs,
    lrr,
    wg_own,
    wg_snd,
    wg_rcv,
    ggu,
    gd,
    ag_send,
    ag_recv,
    ip_send,
    ip_recv,
    rt_send,
    rt_recv,
    nr_send,
    nr_recv,
    fr_send,
    fr_recv,
    lr_send,
    lr_recv,
    wx_send,
    wx_recv,
    w_sem,
    o_sem,
):
    B, D = tok_ref.shape
    H = wd.shape[1]
    W2 = D + EXTRA
    half = Z // 2
    quarter = Z // 4
    R = quarter * CAP
    rows = G * R
    nt = quarter * B
    side = 4 if G == 16 else 0

    s = lax.axis_index("seq")
    e = lax.axis_index("expert")
    z = e // 2
    c = e % 2
    q = e // (Z * 2 // 4)
    expert = s * 4 + q
    partner = (s, z * 2 + 1 - c)

    def along(k):
        return (s, lax.rem(z + Z + k, Z) * 2 + c)

    def ahead(i):
        if side:
            return lax.rem(s // side + i // side, side) * side + lax.rem(s % side + i % side, side)
        return lax.rem(s + i, G)

    def behind(i):
        if side:
            return lax.rem(s // side + side - i // side, side) * side + lax.rem(
                s % side + side - i % side, side
            )
        return lax.rem(s + G - i, G)

    def loop(lo, hi, fn):
        def step(i, carry):
            fn(i)
            return carry

        lax.fori_loop(lo, hi, step, 0)

    def iota(shape, dim):
        return lax.broadcasted_iota(jnp.int32, shape, dim)

    def log2(n):
        return n.bit_length() - 1

    def remote(src, dst, send, recv, to):
        return pltpu.make_async_remote_copy(
            src_ref=src,
            dst_ref=dst,
            send_sem=send,
            recv_sem=recv,
            device_id=to,
            device_id_type=MESH,
        )

    w_copies = [
        pltpu.make_async_copy(wgu_hbm.at[0], wgu.at[c], w_sem.at[0]),
        pltpu.make_async_copy(wd_hbm.at[0], wd.at[c], w_sem.at[1]),
    ]
    for copy in w_copies:
        copy.start()

    barrier = pltpu.get_barrier_semaphore()

    def greet(i):
        pl.semaphore_signal(barrier, inc=1, device_id=(ahead(i), e), device_id_type=MESH)

    loop(1, G, greet)
    for k in GREET:
        pl.semaphore_signal(barrier, inc=1, device_id=along(k), device_id_type=MESH)
    pl.semaphore_signal(barrier, inc=1, device_id=partner, device_id_type=MESH)

    lane = iota((B, EXTRA), 1)
    ids = ids_ref[...].astype(F32)
    probs = probs_ref[...].astype(F32)
    own_meta = jnp.zeros((B, EXTRA), F32)
    for k in range(top):
        own_meta = jnp.where(
            lane == k, jnp.broadcast_to(ids[:, k : k + 1], (B, EXTRA)), own_meta
        )
        own_meta = jnp.where(
            lane == 8 + k, jnp.broadcast_to(probs[:, k : k + 1], (B, EXTRA)), own_meta
        )
    own = POS[0]
    xm[own, :, :D] = tok_ref[...]
    xm[own, :, D:] = own_meta.astype(BF)
    dyb[own] = og_ref[...]

    pl.semaphore_wait(barrier, G - 1 + len(GREET) + 1)

    def ag(way, i, piece):
        buf = xm if piece == 0 else dyb
        src, dst = (-i, -i - 1) if way == 0 else (i, i + 1)
        return remote(
            buf.at[POS[src]],
            buf.at[POS[dst]],
            ag_send.at[way, piece, i],
            ag_recv.at[way, piece, i],
            along(1 if way == 0 else -1),
        )

    last = (half - 1, half - 2)

    def ag_step(i):
        for piece in range(2):
            for way in range(2):
                if 0 <= i - 1 <= last[way]:
                    ag(way, i - 1, piece).wait_recv()
                if i <= last[way]:
                    ag(way, i, piece).start()

    def wx(i):
        src = wgu if i == 0 else wd
        return remote(src.at[c], src.at[c], wx_send.at[i], wx_recv.at[i], partner)

    def wx_in(i):
        src = wgu if i == 0 else wd
        return remote(src.at[1 - c], src.at[1 - c], wx_send.at[i], wx_recv.at[i], partner)

    def ip(n, piece, to, frm):
        return remote(
            sbuf.at[n // 2, piece, n % 2, pl.ds(to * R, R)],
            rbuf.at[n // 2, piece, n % 2, pl.ds(frm * R, R)],
            ip_send.at[n, piece, to],
            ip_recv.at[n, piece, frm],
            (to, e),
        )

    def ip_own(n, piece):
        return pltpu.make_async_copy(
            sbuf.at[n // 2, piece, n % 2, pl.ds(s * R, R)],
            rbuf.at[n // 2, piece, n % 2, pl.ds(s * R, R)],
            ip_send.at[n, piece, s],
        )

    def pick(n):
        blocks = pl.ds(n * quarter, quarter)
        meta = xm[blocks, :, D:].reshape(nt, EXTRA).astype(F32)
        lane_expert = (iota((nt, EXTRA), 1) * 4 + q).astype(F32)
        member = jnp.zeros((nt, EXTRA), F32)
        weight = jnp.zeros((nt, EXTRA), F32)
        for k in range(top):
            hit = jnp.broadcast_to(meta[:, k : k + 1], (nt, EXTRA)) == lane_expert
            member = member + jnp.where(hit, 1.0, 0.0)
            weight = weight + jnp.where(
                hit, jnp.broadcast_to(meta[:, 8 + k : 9 + k], (nt, EXTRA)), 0.0
            )
        member = member.astype(BF)
        weight = weight.astype(BF)
        ti, tj = iota((nt, nt), 0), iota((nt, nt), 1)
        earlier = ((ti >> log2(B)) == (tj >> log2(B))) & (tj < ti)
        rank = dot(jnp.where(earlier, 1.0, 0.0).astype(BF), member, 1, 0).astype(BF)
        spread = jnp.where(
            iota((EXTRA, rows), 0) == (iota((EXTRA, rows), 1) >> log2(R)), 1.0, 0.0
        ).astype(BF)
        member_s = dot(member, spread, 1, 0)
        rank_s = dot(rank, spread, 1, 0)
        weight_s = dot(weight, spread, 1, 0)
        tok, slot = iota((nt, rows), 0), iota((nt, rows), 1)
        mine = (tok >> log2(B)) == ((slot & (R - 1)) >> 1)
        chosen = (member_s > 0.5) & (rank_s == (slot & 1).astype(F32)) & mine
        picked = jnp.where(chosen, 1.0, 0.0).astype(BF)
        pt[n] = picked
        for piece in range(2):
            matrix = picked if piece == 0 else jnp.where(chosen, weight_s, 0.0).astype(BF)
            for at, wide in tiles(D, 512):
                if piece == 0:
                    block = xm[blocks, :, at : at + wide].reshape(nt, wide)
                else:
                    block = dyb[blocks, :, at : at + wide].reshape(nt, wide)
                value = dot(matrix, block, 0, 0).astype(BF)
                sbuf[n // 2, piece, n % 2, :, at : at + wide] = value
            loop(1, G, lambda i: ip(n, piece, ahead(i), s).start())
            ip_own(n, piece).start()

    ag_step(0)
    for copy in w_copies:
        copy.wait()
    for i in range(2):
        wx(i).start()
    for n in range(4):
        ag_step(2 * n + 1)
        ag_step(2 * n + 2)
        pick(n)

    def arrived(n):
        for piece in range(2):
            ip_own(n, piece).wait()

            def one(i):
                frm = behind(i)
                ip(n, piece, frm, frm).wait_recv()

            loop(1, G, one)

    def forward_part(ch):
        x = rbuf[ch, 0].reshape(2 * rows, D)
        dy = rbuf[ch, 1].reshape(2 * rows, D)
        score = jnp.zeros((1, 2 * rows), F32)
        for k in range(2):
            gu = dot(wgu[k].reshape(2 * H, D), x, 1, 1)
            gate, upper = gu[:H], gu[H:]
            err = dot(wd[k], dy, 1, 1)
            sig = jax.nn.sigmoid(gate)
            act = gate * sig * upper
            actt[ch, k] = act.astype(BF)
            ggt[ch, k, :H] = (err * upper * sig * (1.0 + gate * (1.0 - sig))).astype(BF)
            ggt[ch, k, H:] = (err * gate * sig).astype(BF)
            score = score + jnp.sum(err * act, axis=0, keepdims=True)
        score = jnp.broadcast_to(score, (16, 2 * rows)).astype(BF)
        mark = (iota((16, EXTRA), 0) == 0) & (iota((16, EXTRA), 1) == expert)
        value = dot(score, jnp.where(mark, 1.0, 0.0).astype(BF), 0, 0)
        rts[ch, :, :, D:] = value.astype(BF).reshape(2, rows, EXTRA)

    def rt(ch, p, to, frm):
        at, wide = pieces[ch][p]
        return remote(
            rts.at[ch, :, pl.ds(to * R, R), pl.ds(at, wide)],
            rtr.at[ch, :, pl.ds(frm * R, R), pl.ds(at, wide)],
            rt_send.at[ch, p, to],
            rt_recv.at[ch, p, frm],
            (to, e),
        )

    def rt_own(ch, p):
        at, wide = pieces[ch][p]
        return pltpu.make_async_copy(
            rts.at[ch, :, pl.ds(s * R, R), pl.ds(at, wide)],
            rtr.at[ch, :, pl.ds(s * R, R), pl.ds(at, wide)],
            rt_send.at[ch, p, s],
        )

    def compute(ch):
        forward_part(ch)
        for p, (first, width) in enumerate(pieces[ch]):
            for at, wide in tiles(min(width, D - first), 512):
                cols = slice(first + at, first + at + wide)
                w = wgu[:, :, :, cols].reshape(4 * H, wide)
                value = dot(ggt[ch].reshape(4 * H, 2 * rows), w, 0, 0)
                rts[ch, :, :, cols] = value.astype(BF).reshape(2, rows, wide)
            loop(1, G, lambda i: rt(ch, p, ahead(i), s).start())
            rt_own(ch, p).start()

    def home(ch, p):
        rt_own(ch, p).wait()

        def one(i):
            frm = behind(i)
            rt(ch, p, frm, frm).wait_recv()

        loop(1, G, one)
        first, width = pieces[ch][p]
        for at, wide in tiles(width, 512):
            cols = slice(first + at, first + at + wide)
            for j in range(2):
                n = 2 * ch + j
                value = dot(pt[n], rtr[ch, j, :, cols], 1, 0)
                tp[n * quarter : (n + 1) * quarter, :, cols] = value.reshape(quarter, B, wide)

    for i in range(2):
        wx_in(i).wait_recv()
    arrived(0)
    arrived(1)
    compute(0)
    arrived(2)
    arrived(3)
    compute(1)

    def near(i):
        return remote(nrs.at[i], nrr.at[i], nr_send.at[i], nr_recv.at[i], along(NEAR[i]))

    home(0, 0)
    for i, rel in enumerate(NEAR):
        nrs[i] = tp[POS[rel]].astype(BF)
        near(i).start()

    def weight_grads(k, put):
        for at, wide in tiles(D, 512):
            cols = slice(at, at + wide)
            total = jnp.zeros((2 * H, wide), F32)
            total_down = jnp.zeros((H, wide), F32)
            for ch in range(2):
                x = rbuf[ch, 0, :, :, cols].reshape(2 * rows, wide)
                dy = rbuf[ch, 1, :, :, cols].reshape(2 * rows, wide)
                total = total + dot(ggt[ch, k], x, 1, 0)
                total_down = total_down + dot(actt[ch, k], dy, 1, 0)
            put[: 2 * H, cols] = total
            put[2 * H :, cols] = total_down

    wg = remote(wg_snd, wg_rcv, wx_send.at[2], wx_recv.at[2], partner)
    weight_grads(1 - c, wg_snd)
    wg.start()
    weight_grads(c, wg_own)

    spans = pieces[1]

    def far(i, p):
        cols = pl.ds(*spans[p])
        return remote(
            frs.at[i, :, cols],
            frr.at[i, :, cols],
            fr_send.at[i, p],
            fr_recv.at[i, p],
            along(FAR[i][0]),
        )

    def final(i, p):
        cols = pl.ds(*spans[p])
        return remote(
            lrs.at[i, :, cols],
            lrr.at[i, :, cols],
            lr_send.at[i, p],
            lr_recv.at[i, p],
            along(LAST[i][0]),
        )

    def second_hop(p):
        cols = slice(spans[p][0], sum(spans[p]))
        for way, (_, rel) in enumerate(LAST):
            total = tp[POS[rel], :, cols]
            for i, (_, _, which) in enumerate(FAR):
                if which == way:
                    far(i, p).wait_recv()
                    total = total + frr[i, :, cols].astype(F32)
            lrs[way, :, cols] = total.astype(BF)
            final(way, p).start()

    for p in range(len(spans)):
        home(1, p)
        cols = slice(spans[p][0], sum(spans[p]))
        for i, (_, rel, _) in enumerate(FAR):
            frs[i, :, cols] = tp[POS[rel], :, cols].astype(BF)
            far(i, p).start()
        if p > 0:
            second_hop(p - 1)
    second_hop(len(spans) - 1)

    wg.wait_recv()
    for at, wide in tiles(D, 512):
        cols = slice(at, at + wide)
        total = (wg_own[:, cols] + wg_rcv[:, cols]).astype(BF)
        ggu[:, :, cols] = total[: 2 * H].reshape(2, H, wide)
        gd[:, cols] = total[2 * H :]
    o_copies = [
        pltpu.make_async_copy(ggu, ggu_hbm.at[0], o_sem.at[0]),
        pltpu.make_async_copy(gd, gd_hbm.at[0], o_sem.at[1]),
    ]
    for copy in o_copies:
        copy.start()

    for i in range(len(NEAR)):
        near(i).wait_recv()
    for p in range(len(spans)):
        first, width = spans[p]
        cols = slice(first, first + width)
        total = tp[own, :, cols]
        for i in range(len(NEAR)):
            total = total + nrr[i, :, cols].astype(F32)
        for way in range(2):
            final(way, p).wait_recv()
            total = total + lrr[way, :, cols].astype(F32)
        if first + width == W2:
            scores = total[:, width - EXTRA :]
            total = total[:, : width - EXTRA]
        gt_ref[:, first : first + total.shape[1]] = total.astype(BF)
    lanes = lane.astype(F32)
    for k in range(top):
        hit = jnp.broadcast_to(ids[:, k : k + 1], (B, EXTRA)) == lanes
        value = jnp.sum(jnp.where(hit, scores, 0.0), axis=1, keepdims=True)
        gp_ref[:, k : k + 1] = value / probs[:, k : k + 1]

    for piece in range(2):
        for way in range(2):
            for i in range(last[way] + 1):
                ag(way, i, piece).wait_send()
    for i in range(2):
        wx(i).wait_send()
    wg.wait_send()
    for n in range(4):
        for piece in range(2):
            loop(1, G, lambda i: ip(n, piece, ahead(i), s).wait_send())
    for ch in range(2):
        for p in range(len(pieces[ch])):
            loop(1, G, lambda i: rt(ch, p, ahead(i), s).wait_send())
    for i in range(len(NEAR)):
        near(i).wait_send()
    for p in range(len(spans)):
        for i in range(len(FAR)):
            far(i, p).wait_send()
        for i in range(len(LAST)):
            final(i, p).wait_send()
    for copy in o_copies:
        copy.wait()


def hand_over(*refs):
    count = (len(refs) - 2) // 3
    ins, outs, held = refs[:count], refs[count : 2 * count], refs[2 * count : 3 * count]
    in_sem, out_sem = refs[-2:]
    reads = [pltpu.make_async_copy(ins[i], held[i], in_sem.at[i]) for i in range(count)]
    writes = [pltpu.make_async_copy(held[i], outs[i], out_sem.at[i]) for i in range(count)]
    for copy in reads:
        copy.start()
    for read, write in zip(reads, writes):
        read.wait()
        write.start()
    for copy in writes:
        copy.wait()


def body(tokens, out_grads, route_ids, route_probs, w_gate_up, w_down):
    B, D = tokens.shape
    top = route_ids.shape[1]
    H = w_down.shape[1]
    G = lax.axis_size("seq")
    Z = lax.axis_size("expert") // 2
    half = Z // 2
    quarter = Z // 4
    rows = G * quarter * CAP
    nt = quarter * B
    W2 = D + EXTRA
    pieces = (((0, W2),), ((0, D // 2), (D // 2, D // 2 + EXTRA)))
    count = max(len(p) for p in pieces)
    vmem = pl.BlockSpec(memory_space=pltpu.VMEM)
    anys = pl.BlockSpec(memory_space=pl.ANY)
    dma = pltpu.SemaphoreType.DMA
    outs = (
        jax.ShapeDtypeStruct((B, D), BF),
        jax.ShapeDtypeStruct((B, top), F32),
        jax.ShapeDtypeStruct(w_gate_up.shape, BF),
        jax.ShapeDtypeStruct(w_down.shape, BF),
    )
    gt, gp, ggu, gd = pl.pallas_call(
        functools.partial(kernel, G, Z, top, pieces),
        out_shape=outs,
        in_specs=[vmem, vmem, vmem, vmem, anys, anys],
        out_specs=(vmem, vmem, anys, anys),
        scratch_shapes=[
            pltpu.VMEM((Z, B, W2), BF),
            pltpu.VMEM((Z, B, D), BF),
            pltpu.VMEM((2, 2, 2, rows, D), BF),
            pltpu.VMEM((2, 2, 2, rows, D), BF),
            pltpu.VMEM((4, nt, rows), BF),
            pltpu.VMEM((2, 2, H, D), BF),
            pltpu.VMEM((2, H, D), BF),
            pltpu.VMEM((2, 2, 2 * H, 2 * rows), BF),
            pltpu.VMEM((2, 2, H, 2 * rows), BF),
            pltpu.VMEM((2, 2, rows, W2), BF),
            pltpu.VMEM((2, 2, rows, W2), BF),
            pltpu.VMEM((Z, B, W2), F32),
            pltpu.VMEM((len(NEAR), B, W2), BF),
            pltpu.VMEM((len(NEAR), B, W2), BF),
            pltpu.VMEM((len(FAR), B, W2), BF),
            pltpu.VMEM((len(FAR), B, W2), BF),
            pltpu.VMEM((len(LAST), B, W2), BF),
            pltpu.VMEM((len(LAST), B, W2), BF),
            pltpu.VMEM((3 * H, D), F32),
            pltpu.VMEM((3 * H, D), F32),
            pltpu.VMEM((3 * H, D), F32),
            pltpu.VMEM((2, H, D), BF),
            pltpu.VMEM((H, D), BF),
            dma((2, 2, half)),
            dma((2, 2, half)),
            dma((4, 2, G)),
            dma((4, 2, G)),
            dma((2, count, G)),
            dma((2, count, G)),
            dma((len(NEAR),)),
            dma((len(NEAR),)),
            dma((len(FAR), count)),
            dma((len(FAR), count)),
            dma((len(LAST), count)),
            dma((len(LAST), count)),
            dma((3,)),
            dma((3,)),
            dma((2,)),
            dma((2,)),
        ],
        compiler_params=pltpu.CompilerParams(
            collective_id=0, has_side_effects=True, vmem_limit_bytes=56 * 1024 * 1024
        ),
        name="moe_backward",
    )(tokens, out_grads, route_ids, route_probs, w_gate_up, w_down)
    gt, ggu, gd = pl.pallas_call(
        hand_over,
        out_shape=(outs[0], outs[2], outs[3]),
        in_specs=[anys] * 3,
        out_specs=(anys,) * 3,
        scratch_shapes=[
            pltpu.VMEM(tokens.shape, BF),
            pltpu.VMEM(w_gate_up.shape, BF),
            pltpu.VMEM(w_down.shape, BF),
            dma((3,)),
            dma((3,)),
        ],
        name="hand_over",
    )(gt, ggu, gd)
    return gt, gp, ggu, gd


def solution(mesh):
    in_specs = (
        P(("seq", "expert"), None),
        P(("seq", "expert"), None),
        P(("seq", "expert"), None),
        P(("seq", "expert"), None),
        P(("seq", "expert"), None, None, None),
        P(("seq", "expert"), None, None),
    )
    out_specs = (
        P(("seq", "expert"), None),
        P(("seq", "expert"), None),
        P(("seq", "expert"), None, None, None),
        P(("seq", "expert"), None, None),
    )
    return jax.shard_map(body, mesh=mesh, in_specs=in_specs, out_specs=out_specs, check_vma=False)
```

time: 154 us -> 129 us (0.84)
  the two profiles are of different devices: /device:TPU:20 before, /device:TPU:70 now
where the time goes in v2:
time: 129 us
  Pallas kernels  125 us (97%)
  local copies, waits for them, and re-layouts  3.39 us (3%)
    pallas_call x1, Pallas kernels, body(): pl.pallas_call(functools.partial(kernel, G, Z, top, pieces), out_shape=ou...  122 us
    unnamed x5, local copies, waits for them, and re-layouts  3.39 us
    pallas_call x1, Pallas kernels, body(): pl.pallas_call(hand_over, out_shape=(outs[0], outs[2], outs[3]), in_specs...  2.79 us

profile of v2, /device:TPU:70, one launch (start us, length us, event | category | flops | bytes accessed | tf_op | source)
XLA Modules:
  0.0 129.1 jit_solution(4582194872260512831)
XLA Ops:
  0.6 1.4 %copy.11.probs_ref = bf16[16,6]{1,0:T(8,128)(2,1)} copy(bf16[16,6]{0,1:T(8,128)(2,1)} %param.9) | data formatting | bytes 384 | tf_op args[3]
  2.0 1.4 %copy.10.ids_ref = s32[16,6]{1,0:T(8,128)} copy(s32[16,6]{0,1:T(8,128)} %param.8) | data formatting | bytes 768 | tf_op args[2]
  3.3 122.3 %moe_backward.1 = (bf16[16,2048]{1,0:T(8,128)(2,1)}, f32[16,6]{1,0:T(8,128)}, bf16[1,2,176,2048]{3,2,1,0:T(8,128)(2,1)}, bf16[1,176,2048]{2,1,0:T(8,128)(2,1)}) custom-call(bf16[16,2048]{1,0:T(8,128)(2,1)} %tok_ref.1, bf16[16,2048]{1,0:T(8,128)(2,1)} %og_ref.1, s32[16,6]{1,0:T(8,128)} %copy.10.ids_ref, bf16[16,6]{1,0:T(8,128)(2,1)} %copy.11.probs_ref, ...), custom_call_target="tpu_custom_call" | custom-call | tf_op jit(solution)/shard_map/moe_backward/pallas_call | solution.py:521
  125.6 0.0 copy-start
  125.7 2.8 %hand_over.1 = (bf16[16,2048]{1,0:T(8,128)(2,1)}, bf16[1,2,176,2048]{3,2,1,0:T(8,128)(2,1)}, bf16[1,176,2048]{2,1,0:T(8,128)(2,1)}) custom-call(bf16[16,2048]{1,0:T(8,128)(2,1)} %get-tuple-element.11.refs_0_, bf16[1,2,176,2048]{3,2,1,0:T(8,128)(2,1)} %get-tuple-element.12.refs_1_, bf16[1,176,2048]{2,1,0:T(8,128)(2,1)} %get-tuple-element.13.refs_2_), custom_call_target="tpu_custom_call" | custom-call | tf_op jit(solution)/shard_map/hand_over/pallas_call | solution.py:572
  128.5 0.0 copy-done
  128.5 0.7 copy.12
Async XLA Ops:
  125.6 2.8 %copy-start = (f32[16,6]{1,0:T(8,128)S(1)}, f32[16,6]{1,0:T(8,128)}, u32[]{:S(2)}) copy-start(f32[16,6]{1,0:T(8,128)} %get-tuple-element.19) | copy-start | bytes 1156

commit v3 on v2

--- a/solution.py
+++ b/solution.py
@@ -106,24 +106,14 @@
     def along(k):
         return (s, lax.rem(z + Z + k, Z) * 2 + c)
 
-    def ahead(i):
-        if side:
-            return lax.rem(s // side + i // side, side) * side + lax.rem(s % side + i % side, side)
-        return lax.rem(s + i, G)
-
-    def behind(i):
-        if side:
-            return lax.rem(s // side + side - i // side, side) * side + lax.rem(
-                s % side + side - i % side, side
-            )
-        return lax.rem(s + G - i, G)
-
-    def loop(lo, hi, fn):
-        def step(i, carry):
-            fn(i)
-            return carry
-
-        lax.fori_loop(lo, hi, step, 0)
+    if side:
+        ys = [lax.rem(s // side + k, side) * side for k in range(side)]
+        xs = [lax.rem(s % side + k, side) for k in range(side)]
+        ahead = [ys[i // side] + xs[i % side] for i in range(G)]
+        behind = [ys[-(i // side) % side] + xs[-(i % side) % side] for i in range(G)]
+    else:
+        ahead = [lax.rem(s + i, G) for i in range(G)]
+        behind = [lax.rem(s + G - i, G) for i in range(G)]
 
     def iota(shape, dim):
         return lax.broadcasted_iota(jnp.int32, shape, dim)
@@ -150,25 +140,17 @@
 
     barrier = pltpu.get_barrier_semaphore()
 
-    def greet(i):
-        pl.semaphore_signal(barrier, inc=1, device_id=(ahead(i), e), device_id_type=MESH)
-
-    loop(1, G, greet)
+    for i in range(1, G):
+        pl.semaphore_signal(barrier, inc=1, device_id=(ahead[i], e), device_id_type=MESH)
     for k in GREET:
         pl.semaphore_signal(barrier, inc=1, device_id=along(k), device_id_type=MESH)
     pl.semaphore_signal(barrier, inc=1, device_id=partner, device_id_type=MESH)
 
-    lane = iota((B, EXTRA), 1)
-    ids = ids_ref[...].astype(F32)
-    probs = probs_ref[...].astype(F32)
-    own_meta = jnp.zeros((B, EXTRA), F32)
-    for k in range(top):
-        own_meta = jnp.where(
-            lane == k, jnp.broadcast_to(ids[:, k : k + 1], (B, EXTRA)), own_meta
-        )
-        own_meta = jnp.where(
-            lane == 8 + k, jnp.broadcast_to(probs[:, k : k + 1], (B, EXTRA)), own_meta
-        )
+    def placed(ref, first):
+        lanes = jnp.where(iota((top, EXTRA), 1) == iota((top, EXTRA), 0) + first, 1.0, 0.0)
+        return dot(ref[...].astype(BF), lanes.astype(BF), 0, 0)
+
+    own_meta = placed(ids_ref, 0) + placed(probs_ref, 8)
     own = POS[0]
     xm[own, :, :D] = tok_ref[...]
     xm[own, :, D:] = own_meta.astype(BF)
@@ -205,12 +187,12 @@
         src = wgu if i == 0 else wd
         return remote(src.at[1 - c], src.at[1 - c], wx_send.at[i], wx_recv.at[i], partner)
 
-    def ip(n, piece, to, frm):
+    def ip(n, piece, i, to, frm):
         return remote(
             sbuf.at[n // 2, piece, n % 2, pl.ds(to * R, R)],
             rbuf.at[n // 2, piece, n % 2, pl.ds(frm * R, R)],
-            ip_send.at[n, piece, to],
-            ip_recv.at[n, piece, frm],
+            ip_send.at[n, piece, i],
+            ip_recv.at[n, piece, i],
             (to, e),
         )
 
@@ -218,7 +200,7 @@
         return pltpu.make_async_copy(
             sbuf.at[n // 2, piece, n % 2, pl.ds(s * R, R)],
             rbuf.at[n // 2, piece, n % 2, pl.ds(s * R, R)],
-            ip_send.at[n, piece, s],
+            ip_send.at[n, piece, 0],
         )
 
     def pick(n):
@@ -258,7 +240,8 @@
                     block = dyb[blocks, :, at : at + wide].reshape(nt, wide)
                 value = dot(matrix, block, 0, 0).astype(BF)
                 sbuf[n // 2, piece, n % 2, :, at : at + wide] = value
-            loop(1, G, lambda i: ip(n, piece, ahead(i), s).start())
+            for i in range(1, G):
+                ip(n, piece, i, ahead[i], s).start()
             ip_own(n, piece).start()
 
     ag_step(0)
@@ -274,12 +257,8 @@
     def arrived(n):
         for piece in range(2):
             ip_own(n, piece).wait()
-
-            def one(i):
-                frm = behind(i)
-                ip(n, piece, frm, frm).wait_recv()
-
-            loop(1, G, one)
+            for i in range(1, G):
+                ip(n, piece, i, behind[i], behind[i]).wait_recv()
 
     def forward_part(ch):
         x = rbuf[ch, 0].reshape(2 * rows, D)
@@ -300,13 +279,13 @@
         value = dot(score, jnp.where(mark, 1.0, 0.0).astype(BF), 0, 0)
         rts[ch, :, :, D:] = value.astype(BF).reshape(2, rows, EXTRA)
 
-    def rt(ch, p, to, frm):
+    def rt(ch, p, i, to, frm):
         at, wide = pieces[ch][p]
         return remote(
             rts.at[ch, :, pl.ds(to * R, R), pl.ds(at, wide)],
             rtr.at[ch, :, pl.ds(frm * R, R), pl.ds(at, wide)],
-            rt_send.at[ch, p, to],
-            rt_recv.at[ch, p, frm],
+            rt_send.at[ch, p, i],
+            rt_recv.at[ch, p, i],
             (to, e),
         )
 
@@ -315,28 +294,26 @@
         return pltpu.make_async_copy(
             rts.at[ch, :, pl.ds(s * R, R), pl.ds(at, wide)],
             rtr.at[ch, :, pl.ds(s * R, R), pl.ds(at, wide)],
-            rt_send.at[ch, p, s],
-        )
-
-    def compute(ch):
-        forward_part(ch)
-        for p, (first, width) in enumerate(pieces[ch]):
-            for at, wide in tiles(min(width, D - first), 512):
-                cols = slice(first + at, first + at + wide)
-                w = wgu[:, :, :, cols].reshape(4 * H, wide)
-                value = dot(ggt[ch].reshape(4 * H, 2 * rows), w, 0, 0)
-                rts[ch, :, :, cols] = value.astype(BF).reshape(2, rows, wide)
-            loop(1, G, lambda i: rt(ch, p, ahead(i), s).start())
-            rt_own(ch, p).start()
+            rt_send.at[ch, p, 0],
+        )
+
+    def row_grads(ch, p):
+        first, width = pieces[ch][p]
+        for at, wide in tiles(min(width, D - first), 512):
+            cols = slice(first + at, first + at + wide)
+            w = wgu[:, :, :, cols].reshape(4 * H, wide)
+            value = dot(ggt[ch].reshape(4 * H, 2 * rows), w, 0, 0)
+            rts[ch, :, :, cols] = value.astype(BF).reshape(2, rows, wide)
+
+    def send_back(ch, p):
+        for i in range(1, G):
+            rt(ch, p, i, ahead[i], s).start()
+        rt_own(ch, p).start()
 
     def home(ch, p):
         rt_own(ch, p).wait()
-
-        def one(i):
-            frm = behind(i)
-            rt(ch, p, frm, frm).wait_recv()
-
-        loop(1, G, one)
+        for i in range(1, G):
+            rt(ch, p, i, behind[i], behind[i]).wait_recv()
         first, width = pieces[ch][p]
         for at, wide in tiles(width, 512):
             cols = slice(first + at, first + at + wide)
@@ -349,18 +326,15 @@
         wx_in(i).wait_recv()
     arrived(0)
     arrived(1)
-    compute(0)
+    forward_part(0)
+    row_grads(0, 0)
+    send_back(0, 0)
     arrived(2)
     arrived(3)
-    compute(1)
-
-    def near(i):
-        return remote(nrs.at[i], nrr.at[i], nr_send.at[i], nr_recv.at[i], along(NEAR[i]))
-
-    home(0, 0)
-    for i, rel in enumerate(NEAR):
-        nrs[i] = tp[POS[rel]].astype(BF)
-        near(i).start()
+    forward_part(1)
+    for p in range(len(pieces[1])):
+        row_grads(1, p)
+        send_back(1, p)
 
     def weight_grads(k, put):
         for at, wide in tiles(D, 512):
@@ -379,6 +353,14 @@
     weight_grads(1 - c, wg_snd)
     wg.start()
     weight_grads(c, wg_own)
+
+    def near(i):
+        return remote(nrs.at[i], nrr.at[i], nr_send.at[i], nr_recv.at[i], along(NEAR[i]))
+
+    home(0, 0)
+    for i, rel in enumerate(NEAR):
+        nrs[i] = tp[POS[rel]].astype(BF)
+        near(i).start()
 
     spans = pieces[1]
 
@@ -451,11 +433,12 @@
             scores = total[:, width - EXTRA :]
             total = total[:, : width - EXTRA]
         gt_ref[:, first : first + total.shape[1]] = total.astype(BF)
-    lanes = lane.astype(F32)
+    lanes = iota((B, EXTRA), 1).astype(F32)
+    meta = xm[own, :, D:].astype(F32)
     for k in range(top):
-        hit = jnp.broadcast_to(ids[:, k : k + 1], (B, EXTRA)) == lanes
+        hit = jnp.broadcast_to(meta[:, k : k + 1], (B, EXTRA)) == lanes
         value = jnp.sum(jnp.where(hit, scores, 0.0), axis=1, keepdims=True)
-        gp_ref[:, k : k + 1] = value / probs[:, k : k + 1]
+        gp_ref[:, k : k + 1] = value / meta[:, 8 + k : 9 + k]
 
     for piece in range(2):
         for way in range(2):
@@ -466,10 +449,12 @@
     wg.wait_send()
     for n in range(4):
         for piece in range(2):
-            loop(1, G, lambda i: ip(n, piece, ahead(i), s).wait_send())
+            for i in range(1, G):
+                ip(n, piece, i, ahead[i], s).wait_send()
     for ch in range(2):
         for p in range(len(pieces[ch])):
-            loop(1, G, lambda i: rt(ch, p, ahead(i), s).wait_send())
+            for i in range(1, G):
+                rt(ch, p, i, ahead[i], s).wait_send()
     for i in range(len(NEAR)):
         near(i).wait_send()
     for p in range(len(spans)):
@@ -568,7 +553,7 @@
             collective_id=0, has_side_effects=True, vmem_limit_bytes=56 * 1024 * 1024
         ),
         name="moe_backward",
-    )(tokens, out_grads, route_ids, route_probs, w_gate_up, w_down)
+    )(tokens, out_grads, route_ids.T, route_probs.T, w_gate_up, w_down)
     gt, ggu, gd = pl.pallas_call(
         hand_over,
         out_shape=(outs[0], outs[2], outs[3]),

time: 129 us -> 124 us (0.961)
  the two profiles are of different devices: /device:TPU:70 before, /device:TPU:8 now
where the time goes in v3:
time: 124 us
  Pallas kernels  123 us (99%)
    pallas_call x1, Pallas kernels, body(): pl.pallas_call(functools.partial(kernel, G, Z, top, pieces), out_shape=ou...  120 us
    pallas_call x1, Pallas kernels, body(): pl.pallas_call(hand_over, out_shape=(outs[0], outs[2], outs[3]), in_specs...  2.79 us

profile of v3, /device:TPU:8, one launch (start us, length us, event | category | flops | bytes accessed | tf_op | source)
XLA Modules:
  0.0 124.3 jit_solution(13326421359409949354)
XLA Ops:
  0.6 120.2 %moe_backward.1 = (bf16[16,2048]{1,0:T(8,128)(2,1)}, f32[16,6]{1,0:T(8,128)}, bf16[1,2,176,2048]{3,2,1,0:T(8,128)(2,1)}, bf16[1,176,2048]{2,1,0:T(8,128)(2,1)}) custom-call(bf16[16,2048]{1,0:T(8,128)(2,1)} %tok_ref.1, bf16[16,2048]{1,0:T(8,128)(2,1)} %og_ref.1, s32[6,16]{1,0:T(8,128)} %bitcast.2, bf16[6,16]{1,0:T(8,128)(2,1)} %bitcast.3, ...), custom_call_target="tpu_custom_call" | custom-call | tf_op jit(solution)/shard_map/moe_backward/pallas_call | solution.py:506
  120.8 0.0 copy-start
  120.8 2.8 %hand_over.1 = (bf16[16,2048]{1,0:T(8,128)(2,1)}, bf16[1,2,176,2048]{3,2,1,0:T(8,128)(2,1)}, bf16[1,176,2048]{2,1,0:T(8,128)(2,1)}) custom-call(bf16[16,2048]{1,0:T(8,128)(2,1)} %get-tuple-element.11.refs_0_, bf16[1,2,176,2048]{3,2,1,0:T(8,128)(2,1)} %get-tuple-element.12.refs_1_, bf16[1,176,2048]{2,1,0:T(8,128)(2,1)} %get-tuple-element.13.refs_2_), custom_call_target="tpu_custom_call" | custom-call | tf_op jit(solution)/shard_map/hand_over/pallas_call | solution.py:557
  123.6 0.0 copy-done
  123.6 0.7 copy.10
Async XLA Ops:
  120.8 2.8 %copy-start = (f32[16,6]{1,0:T(8,128)S(1)}, f32[16,6]{1,0:T(8,128)}, u32[]{:S(2)}) copy-start(f32[16,6]{1,0:T(8,128)} %get-tuple-element.19) | copy-start | bytes 1156

commit v4 on v3

--- a/solution.py
+++ b/solution.py
@@ -329,12 +329,14 @@
     forward_part(0)
     row_grads(0, 0)
     send_back(0, 0)
+    row_grads(0, 1)
     arrived(2)
     arrived(3)
     forward_part(1)
-    for p in range(len(pieces[1])):
+    for p in range(2):
         row_grads(1, p)
         send_back(1, p)
+    send_back(0, 1)
 
     def weight_grads(k, put):
         for at, wide in tiles(D, 512):
@@ -354,15 +356,24 @@
     wg.start()
     weight_grads(c, wg_own)
 
-    def near(i):
-        return remote(nrs.at[i], nrr.at[i], nr_send.at[i], nr_recv.at[i], along(NEAR[i]))
-
-    home(0, 0)
-    for i, rel in enumerate(NEAR):
-        nrs[i] = tp[POS[rel]].astype(BF)
-        near(i).start()
-
     spans = pieces[1]
+
+    def near(i, p):
+        cols = pl.ds(*spans[p])
+        return remote(
+            nrs.at[i, :, cols],
+            nrr.at[i, :, cols],
+            nr_send.at[i, p],
+            nr_recv.at[i, p],
+            along(NEAR[i]),
+        )
+
+    def near_out(p):
+        home(0, p)
+        cols = slice(spans[p][0], sum(spans[p]))
+        for i, rel in enumerate(NEAR):
+            nrs[i, :, cols] = tp[POS[rel], :, cols].astype(BF)
+            near(i, p).start()
 
     def far(i, p):
         cols = pl.ds(*spans[p])
@@ -395,15 +406,19 @@
             lrs[way, :, cols] = total.astype(BF)
             final(way, p).start()
 
-    for p in range(len(spans)):
+    def far_out(p):
         home(1, p)
         cols = slice(spans[p][0], sum(spans[p]))
         for i, (_, rel, _) in enumerate(FAR):
             frs[i, :, cols] = tp[POS[rel], :, cols].astype(BF)
             far(i, p).start()
-        if p > 0:
-            second_hop(p - 1)
-    second_hop(len(spans) - 1)
+
+    near_out(0)
+    far_out(0)
+    far_out(1)
+    second_hop(0)
+    second_hop(1)
+    near_out(1)
 
     wg.wait_recv()
     for at, wide in tiles(D, 512):
@@ -418,17 +433,16 @@
     for copy in o_copies:
         copy.start()
 
-    for i in range(len(NEAR)):
-        near(i).wait_recv()
     for p in range(len(spans)):
         first, width = spans[p]
         cols = slice(first, first + width)
         total = tp[own, :, cols]
-        for i in range(len(NEAR)):
-            total = total + nrr[i, :, cols].astype(F32)
         for way in range(2):
             final(way, p).wait_recv()
             total = total + lrr[way, :, cols].astype(F32)
+        for i in range(len(NEAR)):
+            near(i, p).wait_recv()
+            total = total + nrr[i, :, cols].astype(F32)
         if first + width == W2:
             scores = total[:, width - EXTRA :]
             total = total[:, : width - EXTRA]
@@ -455,9 +469,9 @@
         for p in range(len(pieces[ch])):
             for i in range(1, G):
                 rt(ch, p, i, ahead[i], s).wait_send()
-    for i in range(len(NEAR)):
-        near(i).wait_send()
     for p in range(len(spans)):
+        for i in range(len(NEAR)):
+            near(i, p).wait_send()
         for i in range(len(FAR)):
             far(i, p).wait_send()
         for i in range(len(LAST)):
@@ -492,7 +506,7 @@
     rows = G * quarter * CAP
     nt = quarter * B
     W2 = D + EXTRA
-    pieces = (((0, W2),), ((0, D // 2), (D // 2, D // 2 + EXTRA)))
+    pieces = (((0, D // 2), (D // 2, D // 2 + EXTRA)),) * 2
     count = max(len(p) for p in pieces)
     vmem = pl.BlockSpec(memory_space=pltpu.VMEM)
     anys = pl.BlockSpec(memory_space=pl.ANY)
@@ -538,8 +552,8 @@
             dma((4, 2, G)),
             dma((2, count, G)),
             dma((2, count, G)),
-            dma((len(NEAR),)),
-            dma((len(NEAR),)),
+            dma((len(NEAR), count)),
+            dma((len(NEAR), count)),
             dma((len(FAR), count)),
             dma((len(FAR), count)),
             dma((len(LAST), count)),

time: 124 us -> 122 us (0.984)
  Pallas kernels: 123 us -> 121 us
    pallas_call x1, Pallas kernels: 120 us -> 118 us  [body(): pl.pallas_call(functools.partial(kernel, G, Z, top, pieces), out_shape=ou...]
where the time goes in v4:
time: 122 us
  Pallas kernels  121 us (99%)
    pallas_call x1, Pallas kernels, body(): pl.pallas_call(functools.partial(kernel, G, Z, top, pieces), out_shape=ou...  118 us
    pallas_call x1, Pallas kernels, body(): pl.pallas_call(hand_over, out_shape=(outs[0], outs[2], outs[3]), in_specs...  2.79 us

profile of v4, /device:TPU:8, one launch (start us, length us, event | category | flops | bytes accessed | tf_op | source)
XLA Modules:
  0.0 122.1 jit_solution(9314364734810794687)
XLA Ops:
  0.6 117.9 %moe_backward.1 = (bf16[16,2048]{1,0:T(8,128)(2,1)}, f32[16,6]{1,0:T(8,128)}, bf16[1,2,176,2048]{3,2,1,0:T(8,128)(2,1)}, bf16[1,176,2048]{2,1,0:T(8,128)(2,1)}) custom-call(bf16[16,2048]{1,0:T(8,128)(2,1)} %tok_ref.1, bf16[16,2048]{1,0:T(8,128)(2,1)} %og_ref.1, s32[6,16]{1,0:T(8,128)} %bitcast.2, bf16[6,16]{1,0:T(8,128)(2,1)} %bitcast.3, ...), custom_call_target="tpu_custom_call" | custom-call | tf_op jit(solution)/shard_map/moe_backward/pallas_call | solution.py:520
  118.6 0.0 copy-start
  118.6 2.8 %hand_over.1 = (bf16[16,2048]{1,0:T(8,128)(2,1)}, bf16[1,2,176,2048]{3,2,1,0:T(8,128)(2,1)}, bf16[1,176,2048]{2,1,0:T(8,128)(2,1)}) custom-call(bf16[16,2048]{1,0:T(8,128)(2,1)} %get-tuple-element.11.refs_0_, bf16[1,2,176,2048]{3,2,1,0:T(8,128)(2,1)} %get-tuple-element.12.refs_1_, bf16[1,176,2048]{2,1,0:T(8,128)(2,1)} %get-tuple-element.13.refs_2_), custom_call_target="tpu_custom_call" | custom-call | tf_op jit(solution)/shard_map/hand_over/pallas_call | solution.py:571
  121.4 0.0 copy-done
  121.4 0.7 copy.10
Async XLA Ops:
  118.6 2.8 %copy-start = (f32[16,6]{1,0:T(8,128)S(1)}, f32[16,6]{1,0:T(8,128)}, u32[]{:S(2)}) copy-start(f32[16,6]{1,0:T(8,128)} %get-tuple-element.19) | copy-start | bytes 1156

commit v5 on v4

--- a/solution.py
+++ b/solution.py
@@ -43,8 +43,8 @@
     wd_hbm,
     gt_ref,
     gp_ref,
-    ggu_hbm,
-    gd_hbm,
+    ggu_ref,
+    gd_ref,
     xm,
     dyb,
     sbuf,
@@ -66,8 +66,6 @@
     wg_own,
     wg_snd,
     wg_rcv,
-    ggu,
-    gd,
     ag_send,
     ag_recv,
     ip_send,
@@ -83,7 +81,6 @@
     wx_send,
     wx_recv,
     w_sem,
-    o_sem,
 ):
     B, D = tok_ref.shape
     H = wd.shape[1]
@@ -424,15 +421,8 @@
     for at, wide in tiles(D, 512):
         cols = slice(at, at + wide)
         total = (wg_own[:, cols] + wg_rcv[:, cols]).astype(BF)
-        ggu[:, :, cols] = total[: 2 * H].reshape(2, H, wide)
-        gd[:, cols] = total[2 * H :]
-    o_copies = [
-        pltpu.make_async_copy(ggu, ggu_hbm.at[0], o_sem.at[0]),
-        pltpu.make_async_copy(gd, gd_hbm.at[0], o_sem.at[1]),
-    ]
-    for copy in o_copies:
-        copy.start()
-
+        ggu_ref[0, :, :, cols] = total[: 2 * H].reshape(2, H, wide)
+        gd_ref[0, :, cols] = total[2 * H :]
     for p in range(len(spans)):
         first, width = spans[p]
         cols = slice(first, first + width)
@@ -476,23 +466,6 @@
             far(i, p).wait_send()
         for i in range(len(LAST)):
             final(i, p).wait_send()
-    for copy in o_copies:
-        copy.wait()
-
-
-def hand_over(*refs):
-    count = (len(refs) - 2) // 3
-    ins, outs, held = refs[:count], refs[count : 2 * count], refs[2 * count : 3 * count]
-    in_sem, out_sem = refs[-2:]
-    reads = [pltpu.make_async_copy(ins[i], held[i], in_sem.at[i]) for i in range(count)]
-    writes = [pltpu.make_async_copy(held[i], outs[i], out_sem.at[i]) for i in range(count)]
-    for copy in reads:
-        copy.start()
-    for read, write in zip(reads, writes):
-        read.wait()
-        write.start()
-    for copy in writes:
-        copy.wait()
 
 
 def body(tokens, out_grads, route_ids, route_probs, w_gate_up, w_down):
@@ -511,17 +484,17 @@
     vmem = pl.BlockSpec(memory_space=pltpu.VMEM)
     anys = pl.BlockSpec(memory_space=pl.ANY)
     dma = pltpu.SemaphoreType.DMA
-    outs = (
-        jax.ShapeDtypeStruct((B, D), BF),
-        jax.ShapeDtypeStruct((B, top), F32),
-        jax.ShapeDtypeStruct(w_gate_up.shape, BF),
-        jax.ShapeDtypeStruct(w_down.shape, BF),
+    held = (
+        pltpu.VMEM((B, D), BF),
+        pltpu.VMEM((B, top), F32),
+        pltpu.VMEM(w_gate_up.shape, BF),
+        pltpu.VMEM(w_down.shape, BF),
     )
     gt, gp, ggu, gd = pl.pallas_call(
         functools.partial(kernel, G, Z, top, pieces),
-        out_shape=outs,
+        out_shape=held,
         in_specs=[vmem, vmem, vmem, vmem, anys, anys],
-        out_specs=(vmem, vmem, anys, anys),
+        out_specs=(vmem,) * 4,
         scratch_shapes=[
             pltpu.VMEM((Z, B, W2), BF),
             pltpu.VMEM((Z, B, D), BF),
@@ -544,8 +517,6 @@
             pltpu.VMEM((3 * H, D), F32),
             pltpu.VMEM((3 * H, D), F32),
             pltpu.VMEM((3 * H, D), F32),
-            pltpu.VMEM((2, H, D), BF),
-            pltpu.VMEM((H, D), BF),
             dma((2, 2, half)),
             dma((2, 2, half)),
             dma((4, 2, G)),
@@ -561,27 +532,12 @@
             dma((3,)),
             dma((3,)),
             dma((2,)),
-            dma((2,)),
         ],
         compiler_params=pltpu.CompilerParams(
             collective_id=0, has_side_effects=True, vmem_limit_bytes=56 * 1024 * 1024
         ),
         name="moe_backward",
     )(tokens, out_grads, route_ids.T, route_probs.T, w_gate_up, w_down)
-    gt, ggu, gd = pl.pallas_call(
-        hand_over,
-        out_shape=(outs[0], outs[2], outs[3]),
-        in_specs=[anys] * 3,
-        out_specs=(anys,) * 3,
-        scratch_shapes=[
-            pltpu.VMEM(tokens.shape, BF),
-            pltpu.VMEM(w_gate_up.shape, BF),
-            pltpu.VMEM(w_down.shape, BF),
-            dma((3,)),
-            dma((3,)),
-        ],
-        name="hand_over",
-    )(gt, ggu, gd)
     return gt, gp, ggu, gd
 
 

time: 122 us -> 122 us (level)
  Pallas kernels: 121 us -> 117 us
  local copies, waits for them, and re-layouts: 0.67 us -> 3.25 us
    pallas_call x2 -> x1, Pallas kernels: 121 us -> 117 us  [body(): pl.pallas_call(functools.partial(kernel, G, Z, top, pieces), out_shape=he...]
    unnamed x3, local copies, waits for them, and re-layouts: 0.67 us -> 2.59 us
where the time goes in v5:
time: 122 us; the launch traced here: 121 us
  Pallas kernels  117 us (96%)
  local copies, waits for them, and re-layouts  3.25 us (3%)
    pallas_call x1, Pallas kernels, body(): pl.pallas_call(functools.partial(kernel, G, Z, top, pieces), out_shape=he...  117 us
    unnamed x3, local copies, waits for them, and re-layouts  2.59 us

profile of v5, /device:TPU:8, one launch (start us, length us, event | category | flops | bytes accessed | tf_op | source)
XLA Modules:
  0.0 121.3 jit_solution(5915576040493090330)
XLA Ops:
  0.6 117.4 %moe_backward.1 = (bf16[16,2048]{1,0:T(8,128)(2,1)S(1)}, f32[16,6]{1,0:T(8,128)S(1)}, bf16[1,2,176,2048]{3,2,1,0:T(8,128)(2,1)S(1)}, bf16[1,176,2048]{2,1,0:T(8,128)(2,1)S(1)}) custom-call(bf16[16,2048]{1,0:T(8,128)(2,1)} %tok_ref.1, bf16[16,2048]{1,0:T(8,128)(2,1)} %og_ref.1, s32[6,16]{1,0:T(8,128)} %bitcast.2, bf16[6,16]{1,0:T(8,128)(2,1)} %bitcast.3, ...), custom_call_target="tpu_custom_call" | custom-call | tf_op jit(solution)/shard_map/moe_backward/pallas_call | solution.py:493
  118.1 0.6 copy.14
  118.7 0.7 copy.10
  119.4 0.9 copy.16
  120.2 1.1 copy.15
